TPU v7x, 32 devices: a whole 2x2x4 slice. The times are simulated.
32 devices in a mesh: ground: 16 (over z, x, core), pair: 2 (over y).
Axes of the slice: x: 2, y: 2, z: 4, core: 2. Of those that a mesh axis runs over, the one named last changes fastest.
Arguments:
- coregistered_sweeps: bfloat16 [2, 16, 512, 2, 512], P('pair', 'ground'), may hold values from -6 to 6
- shard_opening_height: int32 [1024], P('ground'), may hold values from 0 to 496
- shard_goal_patch: int32 [1024, 1], P('ground'), may hold values from 0 to 15; in each aligned block of 64 rows (0 to 63, 64 to 127, ...) at most 8 rows name the same one
- shard_patch_place: int32 [1024], P('ground'), may hold values from 0 to 31
Outputs:
- filtered: float32 [2, 1, 16, 2, 64, 64], P('pair', None, 'ground')
Inputs may be any that keep to these rules, and one draw needn't show every extreme that they name: `shard_goal_patch`: among the 64 pieces of the bursts of one ground index, at most 8 name the same ground tile.
All inputs are finite; a program needn't handle non-finite values.
Results may differ from a plain program's by a relative error of at most 0.0023.
Values may be sent and summed in bfloat16 or wider, within the bound.
A program may use at most 320 MiB of HBM per device.

v0:
```python
import math
import jax
import jax.numpy as jnp
from jax import lax
from jax.sharding import PartitionSpec as P

LOOK_ROWS = 4
LOOK_COLS = 16
SHARD_HEIGHT = 16
TILE_ROWS = 256
TILE_COLS = 1024
SWEEP_WIDTH = 512
PATCH_SHARD_LEVEL = 16
SLOTS = 32


def multilook(reference_tiles, secondary_tiles):
    first = reference_tiles.astype(jnp.float32)
    second = secondary_tiles.astype(jnp.float32)
    real_part = first[..., 0, :] * second[..., 0, :] + first[..., 1, :] * second[..., 1, :]
    imag_part = first[..., 1, :] * second[..., 0, :] - first[..., 0, :] * second[..., 1, :]
    joined = jnp.stack([real_part, imag_part], axis=-3)
    leading = joined.shape[:-2]
    row_count = joined.shape[-2]
    col_count = joined.shape[-1]
    boxes = joined.reshape(
        leading + (row_count // LOOK_ROWS, LOOK_ROWS, col_count // LOOK_COLS, LOOK_COLS)
    )
    return jnp.mean(boxes, axis=(-3, -1))


def on_left(matrix, field):
    return jnp.einsum("ij,...jk->...ik", matrix, field, precision=lax.Precision.HIGHEST)


def on_right(field, matrix):
    return jnp.einsum("...ij,jk->...ik", field, matrix, precision=lax.Precision.HIGHEST)


def goldstein(looked):
    length = looked.shape[-1]
    positions = jnp.arange(length, dtype=jnp.int32)
    phase = positions[:, None] * positions[None, :] % length
    angle = phase.astype(jnp.float32) * (2.0 * math.pi / length)
    cosine = jnp.cos(angle)
    sine = jnp.sin(angle)
    real_in = looked[..., 0, :, :]
    imag_in = looked[..., 1, :, :]
    half_real = on_left(cosine, real_in) + on_left(sine, imag_in)
    half_imag = on_left(cosine, imag_in) - on_left(sine, real_in)
    spec_real = on_right(half_real, cosine) + on_right(half_imag, sine)
    spec_imag = on_right(half_imag, cosine) - on_right(half_real, sine)
    weight = (spec_real * spec_real + spec_imag * spec_imag + 1e-06) ** 0.25
    weight = weight / jnp.mean(weight, axis=(-2, -1), keepdims=True)
    spec_real = spec_real * weight
    spec_imag = spec_imag * weight
    back_real = on_left(cosine, spec_real) - on_left(sine, spec_imag)
    back_imag = on_left(cosine, spec_imag) + on_left(sine, spec_real)
    out_real = on_right(back_real, cosine) - on_right(back_imag, sine)
    out_imag = on_right(back_imag, cosine) + on_right(back_real, sine)
    scale = 1.0 / (length * length)
    return jnp.stack([out_real * scale, out_imag * scale], axis=-3)


def partners_of(index, pair_width):
    order = jnp.arange(pair_width, dtype=jnp.int32)
    return order + (order >= index).astype(jnp.int32)


def local(coregistered_sweeps, shard_opening_height, shard_goal_patch, shard_patch_place):
    earth_patch_total_size = lax.axis_size("ground")
    pair_count = lax.axis_size("pair")
    piece_count = shard_opening_height.shape[0]
    place_allowance = max(
        2, (2 * piece_count + earth_patch_total_size - 1) // earth_patch_total_size
    )
    sweep_resident = coregistered_sweeps[0, 0]
    target = shard_goal_patch[:, 0]
    hits = (target[:, None] == jnp.arange(earth_patch_total_size, dtype=jnp.int32)[None, :]).astype(
        jnp.int32
    )
    earlier = jnp.cumsum(hits, axis=0) - hits
    rank = jnp.sum(earlier * hits, axis=1)
    position = target * place_allowance + rank
    matches = (
        position[None, :]
        == jnp.arange(earth_patch_total_size * place_allowance, dtype=jnp.int32)[:, None]
    ).astype(jnp.int32)
    tiles_filled = jnp.sum(matches, axis=1) > 0
    chosen = jnp.sum(matches * jnp.arange(piece_count, dtype=jnp.int32)[None, :], axis=1)
    sweep_height_offset = (
        shard_opening_height[chosen][:, None] + jnp.arange(SHARD_HEIGHT, dtype=jnp.int32)[None, :]
    )
    pieces_to_send = jnp.where(
        tiles_filled[:, None, None, None],
        sweep_resident[sweep_height_offset],
        jnp.zeros((), jnp.bfloat16),
    )
    labels = jnp.where(tiles_filled, shard_patch_place[chosen] + 1, 0).astype(jnp.bfloat16)
    received_pieces, arrived_labels = (
        lax.all_to_all(
            pieces_to_send.reshape(
                earth_patch_total_size, place_allowance, SHARD_HEIGHT, 2, SWEEP_WIDTH
            ),
            "ground",
            split_axis=0,
            concat_axis=0,
            tiled=True,
        ),
        lax.all_to_all(
            labels.reshape(earth_patch_total_size, place_allowance),
            "ground",
            split_axis=0,
            concat_axis=0,
            tiled=True,
        ),
    )
    pieces_flattened = received_pieces.reshape(
        earth_patch_total_size * place_allowance, SHARD_HEIGHT * 2 * SWEEP_WIDTH
    )
    slot_labels = (jnp.arange(SLOTS, dtype=jnp.int32) + 1).astype(jnp.bfloat16)
    selector = arrived_labels.reshape(-1)[None, :] == slot_labels[:, None]
    totals = jnp.dot(
        selector.astype(jnp.bfloat16), pieces_flattened, preferred_element_type=jnp.float32
    )
    counts = jnp.sum(selector.astype(jnp.float32), axis=1)
    smoothed_pixel_mean = (totals / jnp.maximum(counts, 1.0)[:, None]).astype(jnp.bfloat16)
    ground_tile = (
        smoothed_pixel_mean.reshape(PATCH_SHARD_LEVEL, 2, SHARD_HEIGHT, 2, SWEEP_WIDTH)
        .transpose(0, 2, 3, 1, 4)
        .reshape(TILE_ROWS, 2, TILE_COLS)
    )
    pair_width = pair_count - 1
    own_refs = partners_of(lax.axis_index("pair"), pair_width)
    piece = lax.all_gather(ground_tile[None], "pair", axis=0, tiled=True)
    looked_piece = multilook(piece, ground_tile[None])
    indices = jnp.arange(piece.shape[0], dtype=jnp.int32)
    selection = (own_refs[:, None] == indices[None, :]).astype(jnp.float32)
    looked = jnp.einsum("kn,nabc->kabc", selection, looked_piece, precision=lax.Precision.HIGHEST)
    return goldstein(looked)[None, :, None]


def solution(mesh):
    placed = (P("pair", "ground", None, None, None), P("ground"), P("ground", None), P("ground"))
    return jax.shard_map(
        local,
        mesh=mesh,
        in_specs=placed,
        out_specs=P("pair", None, "ground", None, None, None),
        check_vma=False,
    )
```

profile of v0, /device:TPU:0, one launch (start us, length us, event | category | flops | bytes accessed | tf_op | source)
XLA Modules:
  0.0 273.1 jit_solution(14282639509848993935)
XLA Ops:
  6.5 0.8 fusion.16
  7.4 0.8 select_reduce_fusion.1
  8.3 0.7 multiply_add_fusion.1
  9.1 1.6 gather_fusion
  10.7 0.7 convert_element_type.97
  11.4 7.4 %all-to-all-start = ((bf16[16,1,8]{2,1,0:T(2,128)(2,1)}), bf16[16,1,8]{2,1,0:T(2,128)(2,1)S(1)}, u32[]{:S(2)}, u32[]{:S(2)}) async-start(bf16[16,1,8]{2,1,0:T(2,128)(2,1)} %convert_element_type.97), calls=%async_computation | async-start | bytes 16384 | tf_op jit(solution)/shard_map/all_to_all | solution.py:110
  18.8 1.6 gather_fusion.1
  20.6 21.4 %gather_fusion.2 = bf16[2048,2,512]{2,1,0:T(2,128)(2,1)} fusion(bf16[512,2,512]{2,1,0:T(2,128)(2,1)S(1)} %bitcast.86, s32[2048]{0:T(1024)S(1)} %broadcast_clamp_fusion), kind=kCustom, calls=%fused_computation.2 | custom fusion | bytes 8396800 | tf_op jit(solution)/shard_map/gather | solution.py:96
  42.0 7.7 %broadcast_select_fusion = bf16[16,8,16,2,512]{4,3,2,1,0:T(2,128)(2,1)} fusion(bf16[16,8,16,2,512]{4,3,2,1,0:T(2,128)(2,1)} %bitcast.87, pred[16,8]{1,0:T(8,128)(4,1)S(1)} %gt.20), kind=kLoop, calls=%fused_computation.8 | loop fusion | flops 2097152 | bytes 8388736 | tf_op jit(solution)/shard_map/jit(_where)/select_n | solution.py:94
  49.7 6.1 %all-to-all-start.1 = ((bf16[16,8,16,2,512]{4,3,2,1,0:T(2,128)(2,1)}), bf16[16,8,16,2,512]{4,3,2,1,0:T(2,128)(2,1)}, u32[]{:S(2)}, u32[]{:S(2)}) async-start(bf16[16,8,16,2,512]{4,3,2,1,0:T(2,128)(2,1)} %broadcast_select_fusion), calls=%async_computation.1 | async-start | bytes 8388608 | tf_op jit(solution)/shard_map/all_to_all | solution.py:101
  56.4 77.1 %all-to-all-done.1 = bf16[16,8,16,2,512]{4,3,2,1,0:T(2,128)(2,1)} async-done(((bf16[16,8,16,2,512]{4,3,2,1,0:T(2,128)(2,1)}), bf16[16,8,16,2,512]{4,3,2,1,0:T(2,128)(2,1)}, u32[]{:S(2)}, u32[]{:S(2)}) %all-to-all-start.1) | async-done | bytes 4194336 | tf_op jit(solution)/shard_map/all_to_all | solution.py:101
  133.5 7.8 %reshape.291 = bf16[128,16384]{1,0:T(8,128)(2,1)} reshape(bf16[16,8,16,2,512]{4,3,2,1,0:T(2,128)(2,1)} %all-to-all-done.1) | data formatting | bytes 8388608 | tf_op jit(solution)/shard_map/reshape | solution.py:118
  141.3 2.9 %fusion = bf16[32,16384]{1,0:T(8,128)(2,1)S(1)} fusion(bf16[128,16384]{1,0:T(8,128)(2,1)} %reshape.291, f32[32]{0:T(128)S(1)} %broadcast_maximum_fusion, bf16[128]{0:T(256)(128)(2,1)S(1)} %eq.62, bf16[32]{0:T(256)(128)(2,1)S(1)} %add_convert_fusion), kind=kOutput, calls=%fused_computation.5 | convolution fusion | flops 135270400 | bytes 5243328 | tf_op jit(solution)/shard_map/dot_general | solution.py:123
  144.2 0.8 reshape.292
  145.0 1.1 copy.19
  146.1 1.6 broadcast_in_dim_reshape.2
  147.7 1.4 fusion.126
  149.1 4.8 %mul.253 = f32[64,4,64,16]{3,2,1,0:T(8,128)} reshape(f32[1,256,1,1024]{3,1,2,0:T(8,128)S(1)} %get-tuple-element.11) | data formatting | bytes 2097152 | tf_op jit(solution)/shard_map/mul | solution.py:20
  154.0 4.8 %mul.256 = f32[64,4,64,16]{3,2,1,0:T(8,128)} reshape(f32[1,256,1,1024]{3,1,2,0:T(8,128)S(1)} %get-tuple-element.12) | data formatting | bytes 2097152 | tf_op jit(solution)/shard_map/mul | solution.py:20
  158.8 37.1 %all-gather.2.cloned.1.call-done = bf16[2,256,2,1024]{3,1,2,0:T(8,128)(2,1)} async-done(((bf16[1,256,2,1024]{3,1,2,0:T(8,128)(2,1)}), bf16[2,256,2,1024]{3,1,2,0:T(8,128)(2,1)}) %all-gather.2.cloned.1.call-update) | async-done | bytes 2097168 | tf_op jit(solution)/shard_map/all_gather | solution.py:135
  195.9 3.4 %fusion.125 = (f32[2,256,1,1024]{3,1,2,0:T(8,128)S(1)}, f32[2,256,1,1024]{3,1,2,0:T(8,128)}) fusion(bf16[2,256,2,1024]{3,1,2,0:T(8,128)(2,1)} %all-gather.2.cloned.1.call-done), kind=kLoop, calls=%fused_computation.149 | loop fusion | bytes 8388608 | tf_op jit(solution)/shard_map/slice | solution.py:20
  199.3 10.4 %squeeze.10 = f32[2,1,64,4,64,16]{5,4,3,2,0,1:T(8,128)} reshape(f32[2,256,1,1024]{3,1,2,0:T(8,128)} %get-tuple-element.10) | data formatting | bytes 4194304 | tf_op jit(solution)/shard_map/squeeze | solution.py:20
  209.7 9.0 %squeeze.11 = f32[2,1,64,4,64,16]{5,4,3,2,0,1:T(8,128)} reshape(f32[2,256,1,1024]{3,1,2,0:T(8,128)S(1)} %get-tuple-element.9) | data formatting | bytes 4194304 | tf_op jit(solution)/shard_map/squeeze | solution.py:20
  218.7 27.0 %multiply_add_fusion = (f32[2,1,64,4,64,16]{5,4,3,2,0,1:T(8,128)}, f32[2,1,64,4,64,16]{5,4,3,2,0,1:T(8,128)}) fusion(f32[2,1,64,4,64,16]{5,4,3,2,0,1:T(8,128)} %squeeze.11, f32[2,1,64,4,64,16]{5,4,3,2,0,1:T(8,128)} %squeeze.10, f32[64,4,64,16]{3,2,1,0:T(8,128)} %mul.256, f32[64,4,64,16]{3,2,1,0:T(8,128)} %mul.253), kind=kLoop, calls=%fused_computation.7 | loop fusion | flops 3145728 | bytes 10485760 | tf_op jit(solution)/shard_map/add | solution.py:20
  245.7 13.0 %maximum_reduce_fusion = f32[2,2,64,64]{3,2,0,1:T(8,128)S(1)} fusion(f32[2,1,64,4,64,16]{5,4,3,2,0,1:T(8,128)} %get-tuple-element.8, f32[2,1,64,4,64,16]{5,4,3,2,0,1:T(8,128)} %get-tuple-element.7), kind=kLoop, calls=%fused_computation.3 | loop fusion | flops 2080768 | bytes 4259840 | tf_op jit(solution)/shard_map/reduce_sum | solution.py:29
  258.8 0.4 fusion.9
  261.4 0.9 fusion.51
  263.0 0.3 fusion.30
  263.3 0.3 fusion.26
  263.7 0.3 fusion.6
  264.3 0.3 fusion.5
  265.6 0.6 maximum_bitcast_fusion
  (34 shorter events, 4.5 us)
Async XLA Ops:
  6.5 14.1 %copy-start = (bf16[1,1,512,2,512]{4,3,2,1,0:T(2,128)(2,1)S(1)}, bf16[1,1,512,2,512]{4,3,2,1,0:T(2,128)(2,1)}, u32[]{:S(2)}) copy-start(bf16[1,1,512,2,512]{4,3,2,1,0:T(2,128)(2,1)} %param.4) | copy-start | bytes 3145732
  11.4 38.4 %all-to-all-start = ((bf16[16,1,8]{2,1,0:T(2,128)(2,1)}), bf16[16,1,8]{2,1,0:T(2,128)(2,1)S(1)}, u32[]{:S(2)}, u32[]{:S(2)}) async-start(bf16[16,1,8]{2,1,0:T(2,128)(2,1)} %convert_element_type.97), calls=%async_computation | async-start | bytes 16384 | tf_op jit(solution)/shard_map/all_to_all | solution.py:110
  49.7 83.7 %all-to-all-start.1 = ((bf16[16,8,16,2,512]{4,3,2,1,0:T(2,128)(2,1)}), bf16[16,8,16,2,512]{4,3,2,1,0:T(2,128)(2,1)}, u32[]{:S(2)}, u32[]{:S(2)}) async-start(bf16[16,8,16,2,512]{4,3,2,1,0:T(2,128)(2,1)} %broadcast_select_fusion), calls=%async_computation.1 | async-start | bytes 8388608 | tf_op jit(solution)/shard_map/all_to_all | solution.py:101
  55.8 140.1 %all-gather.2.cloned.1.call-start = ((), (), s32[]{:S(2)}) async-start(), calls=%async_computation.2 | async-start | bytes 3145728 | tf_op jit(solution)/shard_map/all_gather | solution.py:135
  245.7 20.5 %copy-start.1 = (bf16[1,1,512,2,512]{4,3,2,1,0:T(2,128)(2,1)S(1)}, bf16[1,1,512,2,512]{4,3,2,1,0:T(2,128)(2,1)}, u32[]{:S(2)}) copy-start(bf16[1,1,512,2,512]{4,3,2,1,0:T(2,128)(2,1)} %param.4) | copy-start | bytes 3145732
Sparse Core Ops, SparseCore 0:
  147.8 48.0 all-gather.1
where the time goes:
time: 274 us; the launch traced here: 273 us
  waiting for transfers between devices  114 us (42%)
  local copies, waits for them, and re-layouts  70.7 us (26%)
  other arithmetic  51.2 us (19%)
  between operations  14.3 us (5%)
  starting transfers between devices  13.6 us (5%)
  matrix products  8.98 us (3%)
    all_to_all x1, waiting for transfers between devices, local(): lax.all_to_all(pieces_to_send.reshape(earth_patch_total_size, place_allow...  77.1 us
    all_gather x1, waiting for transfers between devices, local(): piece = lax.all_gather(ground_tile[None], 'pair', axis=0, tiled=True)  37.1 us
    add x1, other arithmetic, multilook(): first[..., 0, :] * second[..., 0, :] + first[..., 1, :] * second[..., 1, :]  27 us
    gather x1, local copies, waits for them, and re-layouts, local(): sweep_resident[sweep_height_offset]  21.4 us
    reduce_sum x1, other arithmetic, multilook(): return jnp.mean(boxes, axis=(-3, -1))  13 us
    squeeze x1, local copies, waits for them, and re-layouts, multilook(): first[..., 0, :] * second[..., 0, :] + first[..., 1, :] * second[..., 1, :]  10.4 us
    squeeze x1, local copies, waits for them, and re-layouts, multilook(): first[..., 1, :] * second[..., 1, :]  8.98 us
    reshape x1, local copies, waits for them, and re-layouts, local(): received_pieces.reshape(earth_patch_total_size * place_allowance, SHARD_H...  7.8 us
  transfers between devices with their start and end apart: 3, of which 2 were waited for; matrix products, arithmetic and copies ran while one was open for 16% of the time, Pallas kernels for 0%

commit v1 on v0

--- a/solution.py
+++ b/solution.py
@@ -12,6 +12,23 @@
 SWEEP_WIDTH = 512
 PATCH_SHARD_LEVEL = 16
 SLOTS = 32
+
+
+def in_order(tiles, dim):
+    shape = list(tiles.shape[1:])
+    shape[dim] *= tiles.shape[0]
+    return jnp.moveaxis(tiles, 0, dim).reshape(shape)
+
+
+def doubled(x, axis):
+    devices, place = (lax.axis_size(axis), lax.axis_index(axis))
+    blocks, distance = (x[None], 1)
+    while distance < devices:
+        other = lax.ppermute(blocks, axis, [(i, i ^ distance) for i in range(devices)])
+        low = place & distance == 0
+        blocks = jnp.concatenate([jnp.where(low, blocks, other), jnp.where(low, other, blocks)])
+        distance *= 2
+    return blocks
 
 
 def multilook(reference_tiles, secondary_tiles):
@@ -132,7 +149,7 @@
     )
     pair_width = pair_count - 1
     own_refs = partners_of(lax.axis_index("pair"), pair_width)
-    piece = lax.all_gather(ground_tile[None], "pair", axis=0, tiled=True)
+    piece = in_order(doubled(ground_tile[None], "pair"), 0)
     looked_piece = multilook(piece, ground_tile[None])
     indices = jnp.arange(piece.shape[0], dtype=jnp.int32)
     selection = (own_refs[:, None] == indices[None, :]).astype(jnp.float32)

time: 274 us -> 253 us (0.923)
  the two profiles are of different devices: /device:TPU:0 before, /device:TPU:14 now
where the time goes in v1:
time: 253 us; the launch traced here: 252 us
  waiting for transfers between devices  103 us (41%)
  local copies, waits for them, and re-layouts  71.3 us (28%)
  other arithmetic  55.6 us (22%)
  starting transfers between devices  12.9 us (5%)
  matrix products  8.98 us (4%)
    all_to_all x1, waiting for transfers between devices, local(): lax.all_to_all(pieces_to_send.reshape(earth_patch_total_size, place_allow...  92 us
    add x1, other arithmetic, multilook(): first[..., 0, :] * second[..., 0, :] + first[..., 1, :] * second[..., 1, :]  27 us
    gather x1, local copies, waits for them, and re-layouts, local(): sweep_resident[sweep_height_offset]  21.4 us
    reduce_sum x1, other arithmetic, multilook(): return jnp.mean(boxes, axis=(-3, -1))  13 us
    ppermute x1, waiting for transfers between devices, doubled(): lax.ppermute(blocks, axis, [(i, i ^ distance) for i in range(devices)])  10.8 us
    squeeze x1, local copies, waits for them, and re-layouts, multilook(): first[..., 0, :] * second[..., 0, :] + first[..., 1, :] * second[..., 1, :]  10.4 us
    squeeze x1, local copies, waits for them, and re-layouts, multilook(): first[..., 1, :] * second[..., 1, :]  8.98 us
    reshape x1, local copies, waits for them, and re-layouts, local(): received_pieces.reshape(earth_patch_total_size * place_allowance, SHARD_H...  7.8 us
  transfers between devices with their start and end apart: 3, of which 2 were waited for; matrix products, arithmetic and copies ran while one was open for 18% of the time, Pallas kernels for 0%

profile of v1, /device:TPU:14, one launch (start us, length us, event | category | flops | bytes accessed | tf_op | source)
XLA Modules:
  0.0 252.3 jit_solution(16293714407886478182)
XLA Ops:
  0.0 0.8 fusion.17
  0.9 0.8 select_reduce_fusion.1
  1.8 0.7 multiply_add_fusion.1
  2.5 1.6 gather_fusion
  4.1 0.7 convert_element_type.107
  4.8 6.2 %all-to-all-start = ((bf16[16,1,8]{2,1,0:T(2,128)(2,1)}), bf16[16,1,8]{2,1,0:T(2,128)(2,1)S(1)}, u32[]{:S(2)}, u32[]{:S(2)}) async-start(bf16[16,1,8]{2,1,0:T(2,128)(2,1)} %convert_element_type.107), calls=%async_computation | async-start | bytes 16384 | tf_op jit(solution)/shard_map/all_to_all | solution.py:127
  11.1 1.6 gather_fusion.1
  13.0 21.4 %gather_fusion.2 = bf16[2048,2,512]{2,1,0:T(2,128)(2,1)} fusion(bf16[512,2,512]{2,1,0:T(2,128)(2,1)S(1)} %bitcast.94, s32[2048]{0:T(1024)S(1)} %broadcast_clamp_fusion), kind=kCustom, calls=%fused_computation.2 | custom fusion | bytes 8396800 | tf_op jit(solution)/shard_map/gather | solution.py:113
  34.4 7.7 %broadcast_select_fusion = bf16[16,8,16,2,512]{4,3,2,1,0:T(2,128)(2,1)} fusion(bf16[16,8,16,2,512]{4,3,2,1,0:T(2,128)(2,1)} %bitcast.95, pred[16,8]{1,0:T(8,128)(4,1)S(1)} %gt.20), kind=kLoop, calls=%fused_computation.8 | loop fusion | flops 2097152 | bytes 8388736 | tf_op jit(solution)/shard_map/jit(_where)/select_n | solution.py:111
  42.0 6.0 %all-to-all-start.1 = ((bf16[16,8,16,2,512]{4,3,2,1,0:T(2,128)(2,1)}), bf16[16,8,16,2,512]{4,3,2,1,0:T(2,128)(2,1)}, u32[]{:S(2)}, u32[]{:S(2)}) async-start(bf16[16,8,16,2,512]{4,3,2,1,0:T(2,128)(2,1)} %broadcast_select_fusion), calls=%async_computation.1 | async-start | bytes 8388608 | tf_op jit(solution)/shard_map/all_to_all | solution.py:118
  48.4 92.0 %all-to-all-done.1 = bf16[16,8,16,2,512]{4,3,2,1,0:T(2,128)(2,1)} async-done(((bf16[16,8,16,2,512]{4,3,2,1,0:T(2,128)(2,1)}), bf16[16,8,16,2,512]{4,3,2,1,0:T(2,128)(2,1)}, u32[]{:S(2)}, u32[]{:S(2)}) %all-to-all-start.1) | async-done | bytes 4194336 | tf_op jit(solution)/shard_map/all_to_all | solution.py:118
  140.4 7.8 %reshape.296 = bf16[128,16384]{1,0:T(8,128)(2,1)} reshape(bf16[16,8,16,2,512]{4,3,2,1,0:T(2,128)(2,1)} %all-to-all-done.1) | data formatting | bytes 8388608 | tf_op jit(solution)/shard_map/reshape | solution.py:135
  148.2 2.9 %fusion = bf16[32,16384]{1,0:T(8,128)(2,1)S(1)} fusion(bf16[128,16384]{1,0:T(8,128)(2,1)} %reshape.296, f32[32]{0:T(128)S(1)} %broadcast_maximum_fusion, bf16[128]{0:T(256)(128)(2,1)S(1)} %eq.66, bf16[32]{0:T(256)(128)(2,1)S(1)} %add_convert_fusion), kind=kOutput, calls=%fused_computation.5 | convolution fusion | flops 135270400 | bytes 5243328 | tf_op jit(solution)/shard_map/dot_general | solution.py:140
  151.1 0.8 reshape.297
  151.9 2.7 %fusion.126 = (f32[16,16,2,2,512]{4,3,1,0,2:T(2,128)S(1)}, bf16[16,16,2,2,512]{4,3,1,0,2:T(2,128)(2,1)}) fusion(bf16[16,2,16,2,512]{4,3,2,1,0:T(2,128)(2,1)S(1)} %reshape.297), kind=kLoop, calls=%fused_computation.153 | loop fusion | flops 524288 | bytes 4194304 | tf_op jit(solution)/shard_map/convert_element_type | solution.py:36
  154.6 1.8 broadcast_in_dim_broadcast_in_dim_reshape.3
  156.4 0.6 collective-permute-start
  157.0 2.8 %reshape.305 = f32[1,256,2,1024]{3,1,2,0:T(8,128)} reshape(f32[16,16,2,2,512]{4,3,1,0,2:T(2,128)S(1)} %get-tuple-element.15) | data formatting | bytes 4194304 | tf_op jit(solution)/shard_map/convert_element_type | solution.py:36
  159.8 1.7 fusion.128
  161.5 4.8 %mul.253 = f32[64,4,64,16]{3,2,1,0:T(8,128)} reshape(f32[1,256,1,1024]{3,1,2,0:T(8,128)S(1)} %get-tuple-element.11) | data formatting | bytes 2097152 | tf_op jit(solution)/shard_map/mul | solution.py:37
  166.3 4.8 %mul.256 = f32[64,4,64,16]{3,2,1,0:T(8,128)} reshape(f32[1,256,1,1024]{3,1,2,0:T(8,128)S(1)} %get-tuple-element.12) | data formatting | bytes 2097152 | tf_op jit(solution)/shard_map/mul | solution.py:37
  171.2 10.8 %collective-permute-done = bf16[1,1,256,2,1024]{4,2,3,1,0:T(8,128)(2,1)} collective-permute-done((bf16[1,1,256,2,1024]{4,2,3,1,0:T(8,128)(2,1)S(1)}, bf16[1,1,256,2,1024]{4,2,3,1,0:T(8,128)(2,1)}, u32[]{:S(2)}, u32[]{:S(2)}) %collective-permute-start) | collective-permute-done | bytes 1048608 | tf_op jit(solution)/shard_map/ppermute | solution.py:27
  181.9 1.4 broadcast_select_fusion.2
  183.6 1.8 fusion.127
  185.4 10.4 %squeeze.10 = f32[2,1,64,4,64,16]{5,4,3,2,0,1:T(8,128)} reshape(f32[2,256,1,1024]{3,1,2,0:T(8,128)} %get-tuple-element.10) | data formatting | bytes 4194304 | tf_op jit(solution)/shard_map/squeeze | solution.py:37
  195.8 9.0 %squeeze.11 = f32[2,1,64,4,64,16]{5,4,3,2,0,1:T(8,128)} reshape(f32[2,256,1,1024]{3,1,2,0:T(8,128)S(1)} %get-tuple-element.9) | data formatting | bytes 4194304 | tf_op jit(solution)/shard_map/squeeze | solution.py:37
  204.8 27.0 %multiply_add_fusion = (f32[2,1,64,4,64,16]{5,4,3,2,0,1:T(8,128)}, f32[2,1,64,4,64,16]{5,4,3,2,0,1:T(8,128)}) fusion(f32[2,1,64,4,64,16]{5,4,3,2,0,1:T(8,128)} %squeeze.11, f32[2,1,64,4,64,16]{5,4,3,2,0,1:T(8,128)} %squeeze.10, f32[64,4,64,16]{3,2,1,0:T(8,128)} %mul.256, f32[64,4,64,16]{3,2,1,0:T(8,128)} %mul.253), kind=kLoop, calls=%fused_computation.7 | loop fusion | flops 3145728 | bytes 10485760 | tf_op jit(solution)/shard_map/add | solution.py:37
  231.8 13.0 %maximum_reduce_fusion = f32[2,2,64,64]{3,2,0,1:T(8,128)S(1)} fusion(f32[2,1,64,4,64,16]{5,4,3,2,0,1:T(8,128)} %get-tuple-element.8, f32[2,1,64,4,64,16]{5,4,3,2,0,1:T(8,128)} %get-tuple-element.7), kind=kLoop, calls=%fused_computation.3 | loop fusion | flops 2080768 | bytes 4259840 | tf_op jit(solution)/shard_map/reduce_sum | solution.py:46
  244.9 0.4 fusion.10
  247.5 0.9 fusion.52
  249.8 0.3 fusion.7
  251.7 0.6 maximum_bitcast_fusion.1
  (36 shorter events, 5.5 us)
Async XLA Ops:
  0.0 13.0 %copy-start = (bf16[1,1,512,2,512]{4,3,2,1,0:T(2,128)(2,1)S(1)}, bf16[1,1,512,2,512]{4,3,2,1,0:T(2,128)(2,1)}, u32[]{:S(2)}) copy-start(bf16[1,1,512,2,512]{4,3,2,1,0:T(2,128)(2,1)} %param.4) | copy-start | bytes 3145732
  4.8 37.2 %all-to-all-start = ((bf16[16,1,8]{2,1,0:T(2,128)(2,1)}), bf16[16,1,8]{2,1,0:T(2,128)(2,1)S(1)}, u32[]{:S(2)}, u32[]{:S(2)}) async-start(bf16[16,1,8]{2,1,0:T(2,128)(2,1)} %convert_element_type.107), calls=%async_computation | async-start | bytes 16384 | tf_op jit(solution)/shard_map/all_to_all | solution.py:127
  42.0 98.4 %all-to-all-start.1 = ((bf16[16,8,16,2,512]{4,3,2,1,0:T(2,128)(2,1)}), bf16[16,8,16,2,512]{4,3,2,1,0:T(2,128)(2,1)}, u32[]{:S(2)}, u32[]{:S(2)}) async-start(bf16[16,8,16,2,512]{4,3,2,1,0:T(2,128)(2,1)} %broadcast_select_fusion), calls=%async_computation.1 | async-start | bytes 8388608 | tf_op jit(solution)/shard_map/all_to_all | solution.py:118
  156.4 25.5 %collective-permute-start = (bf16[1,1,256,2,1024]{4,2,3,1,0:T(8,128)(2,1)S(1)}, bf16[1,1,256,2,1024]{4,2,3,1,0:T(8,128)(2,1)}, u32[]{:S(2)}, u32[]{:S(2)}) collective-permute-start(bf16[1,1,256,2,1024]{4,2,3,1,0:T(8,128)(2,1)S(1)} %broadcast_in_dim_broadcast_in_dim_reshape.3), channel_id=1, source_target_pairs={{0,1},{1,0},{2,3},{3,2},{4,5},{5,4},{6,7},{7,6},{8,9},{9,8},{10,11... | collective-permute-start | bytes 3145736 | tf_op jit(solution)/shard_map/ppermute | solution.py:27
  231.8 20.5 %copy-start.1 = (bf16[1,1,512,2,512]{4,3,2,1,0:T(2,128)(2,1)S(1)}, bf16[1,1,512,2,512]{4,3,2,1,0:T(2,128)(2,1)}, u32[]{:S(2)}) copy-start(bf16[1,1,512,2,512]{4,3,2,1,0:T(2,128)(2,1)} %param.4) | copy-start | bytes 3145732
